TPU v7x, 512 devices: a whole 4x8x8 slice. The times are simulated.
512 devices in a mesh: src: 128 (over y, z, core), depth: 4 (over x).
Axes of the slice: x: 4, y: 8, z: 8, core: 2. Of those that a mesh axis runs over, the one named last changes fastest.
Arguments:
- incident: float32 [128, 4, 2, 4096], P('src'), may hold values from -6 to 6
- encode: int32 [128], P('src'), may hold values from 0 to 15
- freq_index: int32 [128], P('src'), may hold values from 0 to 7
- wavenum: float32 [8], replicated, may hold values from 1 to 2.8
- slowness: float32 [4, 4096], P('depth'), may hold values from -6 to 6
- probes: bfloat16 [64, 4, 4096], P(None, 'depth'), may hold values from -6 to 6
Outputs:
- sketch_basis: float32 [64, 4, 4096], P(None, 'depth', 'src')
- r_factor: float32 [64, 64], replicated
All inputs are finite; a program needn't handle non-finite values.
Results may differ from a plain program's by a relative error of at most 0.02.
Values may be sent and summed in bfloat16 or wider, within the bound.
A program may use at most 128 MiB of HBM per device.

v0:
```python
import math
import jax
import jax.numpy as jnp
from jax import lax
from jax.sharding import PartitionSpec as P

SIDE = 64
DAMPING = 0.5
STEP_DEPTH = 1.0


def from_behind(x, axis, by):
    size = lax.axis_size(axis)
    pairs = [(i, i + by) for i in range(size) if 0 <= i + by < size]
    return lax.ppermute(x, axis, pairs)


def dft_tables(points, direction):
    counter = jnp.arange(points, dtype=jnp.int32)
    product = counter[:, None] * counter[None, :] % points
    angles = 2.0 * math.pi / points * product.astype(jnp.float32)
    cosine = jnp.cos(angles) / math.sqrt(points)
    sine_part = direction * jnp.sin(angles) / math.sqrt(points)
    matrix = jnp.stack(
        [jnp.stack([cosine, sine_part], axis=1), jnp.stack([-sine_part, cosine], axis=1)], axis=0
    )
    matrix = matrix.astype(jnp.bfloat16)
    total_points = points * points
    twist_index = counter[:, None] * counter[None, :] % total_points
    twist_angle = 2.0 * math.pi / total_points * twist_index.astype(jnp.float32)
    return (matrix, jnp.cos(twist_angle), direction * jnp.sin(twist_angle))


def transform(values, tables):
    matrix, twist_real, twist_imag = tables
    points = matrix.shape[1]
    leading = values.shape[:-2]
    grid_values = values.reshape((-1, 2 * points, points))
    square = matrix.reshape(2 * points, 2 * points)
    segmented = jnp.einsum("nkb,km->nbm", grid_values, square, preferred_element_type=jnp.float32)
    real_part = segmented[:, :, :points]
    imag_part = segmented[:, :, points:]
    turned = jnp.concatenate(
        [
            real_part * twist_real - imag_part * twist_imag,
            real_part * twist_imag + imag_part * twist_real,
        ],
        axis=-1,
    )
    turned = turned.astype(jnp.bfloat16).reshape((-1, points, 2, points))
    result = jnp.einsum("nbsc,sbtd->ntdc", turned, matrix, preferred_element_type=jnp.float32)
    return result.reshape(leading + (2, points * points))


def complex_times(first, second):
    real_part = first[..., 0, :] * second[..., 0, :] - first[..., 1, :] * second[..., 1, :]
    imag_part = first[..., 0, :] * second[..., 1, :] + first[..., 1, :] * second[..., 0, :]
    return jnp.stack([real_part, imag_part], axis=-2)


def conjugate(values):
    return jnp.stack([values[..., 0, :], -values[..., 1, :]], axis=-2)


def propagate(values, spectrum, forward, inverse):
    moved_on = transform(values.astype(jnp.bfloat16), forward)
    return transform(complex_times(moved_on, spectrum).astype(jnp.bfloat16), inverse)


def propagator(wave_nums, points_all):
    counter = jnp.arange(points_all, dtype=jnp.int32)
    folded = jnp.where(counter < points_all // 2, counter, counter - points_all).astype(jnp.float32)
    lateral = 2.0 * math.pi / points_all * folded
    excess = wave_nums[:, None] ** 2 - lateral[None, :] ** 2
    upward = jnp.sqrt(jnp.maximum(excess, 0.0)) * STEP_DEPTH
    damped = jnp.sqrt(jnp.maximum(-excess, 0.0)) * STEP_DEPTH
    real_part = jnp.where(excess > 0, jnp.cos(upward), jnp.exp(-damped))
    imag_part = jnp.where(excess > 0, jnp.sin(upward), jnp.zeros_like(upward))
    return jnp.stack([real_part, imag_part], axis=1)


def screens(wave_nums, slowness):
    phase = wave_nums[:, None, None] * STEP_DEPTH * slowness[None]
    return jnp.stack([jnp.cos(phase), jnp.sin(phase)], axis=2)


def encoded_sources(incident, encode, sources):
    shifts = jnp.arange(sources, dtype=jnp.int32)
    bit_set = encode[:, None] >> shifts[None, :] & 1
    signs_all = (1 - 2 * bit_set).astype(jnp.float32)
    return jnp.sum(signs_all[:, :, None, None] * incident, axis=1)


def lookup_waves(freq_index, wavenum, table_size):
    onehot_rows = (freq_index[:, None] == jnp.arange(table_size, dtype=jnp.int32)[None, :]).astype(
        jnp.float32
    )
    return jnp.sum(onehot_rows * wavenum[None, :], axis=1)


def shards(incident, encode, freq_index, wavenum, slowness, probes):
    points_all = SIDE * SIDE
    forward = dft_tables(SIDE, -1.0)
    inverse = dft_tables(SIDE, 1.0)
    group_count = incident.shape[0]
    plane_count = slowness.shape[0]
    probe_count = probes.shape[0]
    sources = encoded_sources(incident, encode, incident.shape[1])
    wave_nums = lookup_waves(freq_index, wavenum, wavenum.shape[0])
    spectra = propagator(wave_nums, points_all)
    spectra_back = conjugate(spectra)
    plane_screens = screens(wave_nums, slowness)
    born_scale = wave_nums * STEP_DEPTH
    depth_index = lax.axis_index("depth")
    depth_count = lax.axis_size("depth")

    def march_background(upper):
        current = upper
        current = complex_times(plane_screens[:, 0], propagate(current, spectra, forward, inverse))
        states = [current]
        return states

    source_low = sources.astype(jnp.bfloat16)
    received = jnp.zeros_like(source_low)
    for segment in range(depth_count - 1):
        upper = jnp.where(depth_index == 0, source_low, received)
        passing = march_background(upper)
        received = from_behind(passing[-1].astype(jnp.bfloat16), "depth", 1)
    backgrounds = march_background(jnp.where(depth_index == 0, source_low, received))

    def march_tangent(upper, probe_block):
        current = upper
        moved_on = complex_times(
            plane_screens[:, 0][:, None], propagate(current, spectra[:, None], forward, inverse)
        )
        background = backgrounds[0]
        scaled = born_scale[:, None, None] * probe_block[:, 0].astype(jnp.float32)[None]
        born_term = jnp.stack(
            [-scaled * background[:, None, 1], scaled * background[:, None, 0]], axis=2
        )
        current = moved_on + born_term
        return current

    def march_adjoint(lowest_field):
        adjoint = lowest_field
        pieces = [None] * plane_count
        for plane in reversed(range(plane_count)):
            background = backgrounds[plane]
            product_terms = born_scale[:, None, None] * (
                background[:, None, 0] * adjoint[:, :, 1]
                - background[:, None, 1] * adjoint[:, :, 0]
            )
            pieces[plane] = jnp.sum(product_terms, axis=0)
            turned_back = complex_times(conjugate(plane_screens[:, plane])[:, None], adjoint)
            adjoint = propagate(turned_back, spectra_back[:, None], forward, inverse)
        return (adjoint, jnp.stack(pieces, axis=1))

    block_rows = 4
    block_count = probe_count // block_rows
    segment_count = depth_count + block_count - 1
    field_shape = (group_count, block_rows, 2, points_all)
    received_tangent = jnp.zeros(field_shape, jnp.bfloat16)
    bottoms = jnp.zeros((group_count, probe_count + block_rows, 2, points_all), jnp.float32)
    for segment in range(segment_count):
        position = segment - depth_index
        active = (position >= 0) & (position < block_count)
        chosen = jnp.clip(position, 0, block_count - 1)
        slot = jnp.where(active, chosen * block_rows, probe_count)
        probe_block = lax.dynamic_slice_in_dim(probes, chosen * block_rows, block_rows, 0)
        upper = jnp.where(depth_index == 0, jnp.zeros_like(received_tangent), received_tangent)
        lowest = lax.cond(
            active,
            lambda: march_tangent(upper, probe_block),
            lambda: jnp.zeros(field_shape, jnp.float32),
        )
        bottoms = lax.dynamic_update_slice_in_dim(bottoms, lowest, slot, 1)
        if segment + 1 < segment_count:
            received_tangent = from_behind(lowest.astype(jnp.bfloat16), "depth", 1)
    rank_up = depth_count - 1 - depth_index
    received_adjoint = jnp.zeros(field_shape, jnp.float32)
    sketch_part = jnp.zeros((probe_count + block_rows, plane_count, points_all), jnp.float32)
    for segment in range(segment_count):
        position = segment - rank_up
        active = (position >= 0) & (position < block_count)
        chosen = jnp.clip(position, 0, block_count - 1)
        slot = jnp.where(active, chosen * block_rows, probe_count)
        seeded = lax.dynamic_slice_in_dim(bottoms, chosen * block_rows, block_rows, 1)
        lower_field = jnp.where(depth_index == depth_count - 1, seeded, received_adjoint)
        topmost, block_sketch = lax.cond(
            active,
            lambda: march_adjoint(lower_field),
            lambda: (
                jnp.zeros(field_shape, jnp.float32),
                jnp.zeros((block_rows, plane_count, points_all), jnp.float32),
            ),
        )
        sketch_part = lax.dynamic_update_slice_in_dim(sketch_part, block_sketch, slot, 0)
        if segment + 1 < segment_count:
            received_adjoint = from_behind(topmost.astype(jnp.bfloat16), "depth", -1).astype(
                topmost.dtype
            )
    summed = lax.psum_scatter(sketch_part[:probe_count], "src", scatter_dimension=2, tiled=True)
    src_count = lax.axis_size("src")
    slab_width = summed.shape[2]
    local_probes = lax.dynamic_slice_in_dim(
        probes, lax.axis_index("src") * slab_width, slab_width, 2
    ).astype(jnp.float32)
    sketch = summed / (group_count * src_count) + DAMPING * local_probes
    flattened = sketch.reshape(probe_count, plane_count * slab_width)
    row_total = plane_count * slab_width * src_count * depth_count
    gram_local = jnp.dot(flattened, flattened.T, precision=lax.Precision.HIGHEST) / row_total
    gram_matrix = lax.psum(gram_local, ("src", "depth"))
    lower_factor = jnp.linalg.cholesky(gram_matrix)
    identity = jnp.eye(probe_count, dtype=jnp.float32)
    inverse_lower = lax.linalg.triangular_solve(lower_factor, identity, left_side=True, lower=True)
    sketch_basis = jnp.dot(inverse_lower, flattened, precision=lax.Precision.HIGHEST).reshape(
        probe_count, plane_count, slab_width
    )
    return (sketch_basis, lower_factor.T)


def solution(mesh):
    in_specs = (
        P("src", None, None, None),
        P("src"),
        P("src"),
        P(),
        P("depth", None),
        P(None, "depth", None),
    )
    out_specs = (P(None, "depth", "src"), P())
    return jax.shard_map(shards, mesh=mesh, in_specs=in_specs, out_specs=out_specs, check_vma=False)
```

profile of v0, /device:TPU:1, one launch (start us, length us, event | category | flops | bytes accessed | tf_op | source)
XLA Modules:
  0.0 747.9 jit_solution(17268058572091044971)
XLA Ops:
  16.9 3.9 collective-permute-start
  38.6 4.6 conditional.38
  47.1 4.5 conditional.39
  56.7 4.5 conditional.40
  66.3 4.5 conditional.41
  76.5 4.5 conditional.42
  81.1 4.0 collective-permute-start.7
  86.5 4.5 conditional.43
  91.1 4.1 collective-permute-start.8
  96.1 4.5 conditional.44
  105.7 4.5 conditional.45
  115.3 4.5 conditional.46
  124.9 4.5 conditional.47
  134.5 4.5 conditional.48
  144.1 4.5 conditional.49
  153.7 4.5 conditional.50
  163.4 4.5 conditional.51
  173.2 4.4 conditional.52
  177.7 4.2 collective-permute-start.17
  183.2 4.4 conditional.53
  193.1 8.1 %collective-permute-start.19 = (bf16[1,4,2,4096]{3,2,1,0:T(2,128)(2,1)S(1)}, bf16[1,4,2,4096]{3,2,1,0:T(2,128)(2,1)S(1)}, u32[]{:S(2)}, u32[]{:S(2)}) collective-permute-start(bf16[1,4,2,4096]{3,2,1,0:T(2,128)(2,1)S(1)} %get-tuple-element.7639), channel_id=1, source_target_pairs={{0,1},{1,2},{2,3},{4,5},{5,6},{6,7},{8,9},{9,10},{10,11},{12,13},{... | collective-permute-start | bytes 196616 | tf_op jit(solution)/shard_map/ppermute | solution.py:15
  209.3 7.0 collective-permute-done.21
  224.6 17.3 %collective-permute-done.23 = bf16[1,4,2,4096]{3,2,1,0:T(2,128)(2,1)S(1)} collective-permute-done((bf16[1,4,2,4096]{3,2,1,0:T(2,128)(2,1)S(1)}, bf16[1,4,2,4096]{3,2,1,0:T(2,128)(2,1)S(1)}, u32[]{:S(2)}, u32[]{:S(2)}) %collective-permute-start.23) | collective-permute-done | bytes 65568 | tf_op jit(solution)/shard_map/ppermute | solution.py:15
  241.9 3.9 conditional.60
  250.9 3.9 conditional.61
  347.9 4.0 collective-permute-done.35
  360.9 4.0 conditional.73
  370.0 4.2 conditional.74
  385.8 238.3 %reduce-scatter.4.cloned.1.call-done = f32[32,64]{1,0:T(8,128)} async-done(((f32[4096,64]{1,0:T(8,128)}), f32[32,64]{1,0:T(8,128)}) %reduce-scatter.4.cloned.1.call-update) | async-done | bytes 8208
  626.0 99.9 %psum.7 = f32[64,64]{0,1:T(8,128)S(1)} all-reduce(f32[64,64]{0,1:T(8,128)S(1)} %convolution_multiply_fusion), channel_id=1, replica_groups=mesh['src'=128,'depth'=4] {'src','depth'}, use_global_device_ids=true, to_apply=%region_79.80 | all-reduce | flops 4096 | bytes 32768 | tf_op jit(solution)/shard_map/psum | solution.py:212
  726.0 5.8 cholesky.17
  733.2 4.9 custom-call.6
  (1092 shorter events, 367.1 us)
Async XLA Ops:
  7.2 617.0 %reduce-scatter.4.cloned.1.call-start = ((), (), s32[]{:S(2)}) async-start(), calls=%async_computation.1 | async-start | bytes 2113536
  16.9 5.1 collective-permute-start
  51.7 5.0 collective-permute-start.4
  61.3 5.0 collective-permute-start.5
  70.9 5.6 collective-permute-start.6
  81.1 5.3 collective-permute-start.7
  100.7 5.0 collective-permute-start.9
  119.9 5.0 collective-permute-start.11
  139.1 5.0 collective-permute-start.13
  158.3 5.0 collective-permute-start.15
  168.0 5.2 collective-permute-start.16
  177.7 5.5 collective-permute-start.17
  193.1 9.4 %collective-permute-start.19 = (bf16[1,4,2,4096]{3,2,1,0:T(2,128)(2,1)S(1)}, bf16[1,4,2,4096]{3,2,1,0:T(2,128)(2,1)S(1)}, u32[]{:S(2)}, u32[]{:S(2)}) collective-permute-start(bf16[1,4,2,4096]{3,2,1,0:T(2,128)(2,1)S(1)} %get-tuple-element.7639), channel_id=1, source_target_pairs={{0,1},{1,2},{2,3},{4,5},{5,6},{6,7},{8,9},{9,10},{10,11},{12,13},{... | collective-permute-start | bytes 196616 | tf_op jit(solution)/shard_map/ppermute | solution.py:15
  202.6 5.0 collective-permute-start.20
  207.8 8.5 %collective-permute-start.21 = (bf16[1,4,2,4096]{3,2,1,0:T(2,128)(2,1)S(1)}, bf16[1,4,2,4096]{3,2,1,0:T(2,128)(2,1)S(1)}, u32[]{:S(2)}, u32[]{:S(2)}) collective-permute-start(bf16[1,4,2,4096]{3,2,1,0:T(2,128)(2,1)S(1)} %get-tuple-element.4124), channel_id=1, source_target_pairs={{1,0},{2,1},{3,2},{5,4},{6,5},{7,6},{9,8},{10,9},{11,10},{13,12},{... | collective-permute-start | bytes 196616 | tf_op jit(solution)/shard_map/ppermute | solution.py:15
  216.4 5.6 collective-permute-start.22
  222.6 19.2 %collective-permute-start.23 = (bf16[1,4,2,4096]{3,2,1,0:T(2,128)(2,1)S(1)}, bf16[1,4,2,4096]{3,2,1,0:T(2,128)(2,1)S(1)}, u32[]{:S(2)}, u32[]{:S(2)}) collective-permute-start(bf16[1,4,2,4096]{3,2,1,0:T(2,128)(2,1)S(1)} %get-tuple-element.4128), channel_id=1, source_target_pairs={{1,0},{2,1},{3,2},{5,4},{6,5},{7,6},{9,8},{10,9},{11,10},{13,12},{... | collective-permute-start | bytes 196616 | tf_op jit(solution)/shard_map/ppermute | solution.py:15
  245.8 5.0 collective-permute-start.24
  254.8 5.0 collective-permute-start.25
  263.9 5.2 collective-permute-start.26
  273.0 5.3 collective-permute-start.27
  282.4 5.0 collective-permute-start.28
  291.4 5.0 collective-permute-start.29
  300.4 5.0 collective-permute-start.30
  309.4 5.0 collective-permute-start.31
  318.4 5.0 collective-permute-start.32
  327.4 5.0 collective-permute-start.33
  336.4 5.5 collective-permute-start.34
  346.0 5.9 collective-permute-start.35
  355.9 5.0 collective-permute-start.36
  364.9 5.0 collective-permute-start.37
  374.2 5.0 collective-permute-start.38
  (10 other events, 51.9 us)
Sparse Core Ops, SparseCore 0:
  386.0 238.1 reduce-scatter.3
where the time goes:
time: 758 us; the launch traced here: 748 us
  waiting for transfers between devices  339 us (45%)
  starting transfers between devices  104 us (14%)
  blocking collectives  99.9 us (13%)
  other arithmetic  82.9 us (11%)
  local copies, waits for them, and re-layouts  66.5 us (9%)
  matrix products  31.1 us (4%)
  between operations  18.6 us (2%)
    unnamed x2, waiting for transfers between devices  238 us
    ppermute x39, starting transfers between devices, from_behind(): return lax.ppermute(x, axis, pairs)  104 us
    ppermute x39, waiting for transfers between devices, from_behind(): return lax.ppermute(x, axis, pairs)  100 us
    psum x1, blocking collectives, shards(): gram_matrix = lax.psum(gram_local, ('src', 'depth'))  99.9 us
    another operation x16, other arithmetic, march_tangent(): jnp.stack([-scaled * background[:, None, 1], scaled * background[:, None,...  25.4 us
  transfers between devices with their start and end apart: 40, of which 39 were waited for; matrix products, arithmetic and copies ran while one was open for 2% of the time, Pallas kernels for 0%

commit v1 on v0

--- a/solution.py
+++ b/solution.py
@@ -209,7 +209,8 @@
     flattened = sketch.reshape(probe_count, plane_count * slab_width)
     row_total = plane_count * slab_width * src_count * depth_count
     gram_local = jnp.dot(flattened, flattened.T, precision=lax.Precision.HIGHEST) / row_total
-    gram_matrix = lax.psum(gram_local, ("src", "depth"))
+    blocks = lax.all_gather(gram_local, ("src", "depth"), axis=0, tiled=False)
+    gram_matrix = blocks.sum(axis=0)
     lower_factor = jnp.linalg.cholesky(gram_matrix)
     identity = jnp.eye(probe_count, dtype=jnp.float32)
     inverse_lower = lax.linalg.triangular_solve(lower_factor, identity, left_side=True, lower=True)

time: 758 us -> 806 us (1.063)
  waiting for transfers between devices: 339 us -> 479 us
  blocking collectives: 99.9 us -> 0 us
    all_gather x0 -> x1, waiting for transfers between devices: none -> 140 us  [shards(): blocks = lax.all_gather(gram_local, ('src', 'depth'), axis=0, tiled=False)]
    psum x1 -> x0, blocking collectives: 99.9 us -> none  [shards(): gram_matrix = lax.psum(gram_local, ('src', 'depth'))]
    unnamed x2 -> x3, waiting for transfers between devices: 238 us -> 238 us
  transfers between devices with their start and end apart: 40 -> 41, of which waited for: 39 -> 40; matrix products, arithmetic and copies ran while one was open for 2% -> 2% of each run, Pallas kernels for 0% -> 0%
where the time goes in v1:
time: 806 us; the launch traced here: 796 us
  waiting for transfers between devices  479 us (59%)
  starting transfers between devices  104 us (13%)
  other arithmetic  89.7 us (11%)
  local copies, waits for them, and re-layouts  66.5 us (8%)
  matrix products  31.6 us (4%)
  between operations  18.5 us (2%)
    unnamed x3, waiting for transfers between devices  238 us
    all_gather x1, waiting for transfers between devices, shards(): blocks = lax.all_gather(gram_local, ('src', 'depth'), axis=0, tiled=False)  140 us
    ppermute x39, starting transfers between devices, from_behind(): return lax.ppermute(x, axis, pairs)  104 us
    ppermute x39, waiting for transfers between devices, from_behind(): return lax.ppermute(x, axis, pairs)  100 us
    another operation x16, other arithmetic, march_tangent(): jnp.stack([-scaled * background[:, None, 1], scaled * background[:, None,...  25.4 us
  transfers between devices with their start and end apart: 41, of which 40 were waited for; matrix products, arithmetic and copies ran while one was open for 2% of the time, Pallas kernels for 0%

profile of v1, /device:TPU:1, one launch (start us, length us, event | category | flops | bytes accessed | tf_op | source)
XLA Modules:
  0.0 795.6 jit_solution(4947894359978155703)
XLA Ops:
  16.9 3.9 collective-permute-start
  38.6 4.6 conditional.38
  47.1 4.5 conditional.39
  56.7 4.5 conditional.40
  66.3 4.5 conditional.41
  76.5 4.5 conditional.42
  81.1 4.0 collective-permute-start.7
  86.5 4.5 conditional.43
  91.1 4.1 collective-permute-start.8
  96.1 4.5 conditional.44
  105.7 4.5 conditional.45
  115.3 4.5 conditional.46
  124.9 4.5 conditional.47
  134.5 4.5 conditional.48
  144.1 4.5 conditional.49
  153.7 4.5 conditional.50
  163.3 4.5 conditional.51
  173.1 4.4 conditional.52
  177.7 4.2 collective-permute-start.17
  183.2 4.4 conditional.53
  193.1 8.1 %collective-permute-start.19 = (bf16[1,4,2,4096]{3,2,1,0:T(2,128)(2,1)S(1)}, bf16[1,4,2,4096]{3,2,1,0:T(2,128)(2,1)S(1)}, u32[]{:S(2)}, u32[]{:S(2)}) collective-permute-start(bf16[1,4,2,4096]{3,2,1,0:T(2,128)(2,1)S(1)} %get-tuple-element.7639), channel_id=1, source_target_pairs={{0,1},{1,2},{2,3},{4,5},{5,6},{6,7},{8,9},{9,10},{10,11},{12,13},{... | collective-permute-start | bytes 196616 | tf_op jit(solution)/shard_map/ppermute | solution.py:15
  209.2 7.1 collective-permute-done.21
  224.5 17.2 %collective-permute-done.23 = bf16[1,4,2,4096]{3,2,1,0:T(2,128)(2,1)S(1)} collective-permute-done((bf16[1,4,2,4096]{3,2,1,0:T(2,128)(2,1)S(1)}, bf16[1,4,2,4096]{3,2,1,0:T(2,128)(2,1)S(1)}, u32[]{:S(2)}, u32[]{:S(2)}) %collective-permute-start.23) | collective-permute-done | bytes 65568 | tf_op jit(solution)/shard_map/ppermute | solution.py:15
  241.8 3.9 conditional.60
  269.0 3.9 conditional.63
  360.8 4.0 conditional.73
  369.8 4.2 conditional.74
  385.8 238.3 %reduce-scatter.4.cloned.1.call-done = f32[32,64]{1,0:T(8,128)} async-done(((f32[4096,64]{1,0:T(8,128)}), f32[32,64]{1,0:T(8,128)}) %reduce-scatter.4.cloned.1.call-update) | async-done | bytes 8208
  626.6 140.0 %all-gather.3.cloned.1.call-done = f32[32768,64]{1,0:T(8,128)} async-done(((f32[64,64]{1,0:T(8,128)}), f32[32768,64]{1,0:T(8,128)}) %all-gather.3.cloned.1.call-update) | async-done | bytes 8388624 | tf_op jit(solution)/shard_map/all_gather | solution.py:212
  766.6 6.9 reduce_sum.38
  773.7 5.8 cholesky.17
  781.6 4.9 custom-call.6
  (1095 shorter events, 371.6 us)
Async XLA Ops:
  7.2 616.9 %reduce-scatter.4.cloned.1.call-start = ((), (), s32[]{:S(2)}) async-start(), calls=%async_computation.2 | async-start | bytes 2113536
  16.9 5.1 collective-permute-start
  51.7 5.0 collective-permute-start.4
  61.3 5.0 collective-permute-start.5
  70.9 5.6 collective-permute-start.6
  81.1 5.4 collective-permute-start.7
  91.1 5.0 collective-permute-start.8
  100.7 5.0 collective-permute-start.9
  110.3 5.0 collective-permute-start.10
  119.9 5.0 collective-permute-start.11
  129.5 5.0 collective-permute-start.12
  139.1 5.0 collective-permute-start.13
  148.7 5.0 collective-permute-start.14
  158.3 5.0 collective-permute-start.15
  167.9 5.2 collective-permute-start.16
  177.7 5.5 collective-permute-start.17
  193.1 9.4 %collective-permute-start.19 = (bf16[1,4,2,4096]{3,2,1,0:T(2,128)(2,1)S(1)}, bf16[1,4,2,4096]{3,2,1,0:T(2,128)(2,1)S(1)}, u32[]{:S(2)}, u32[]{:S(2)}) collective-permute-start(bf16[1,4,2,4096]{3,2,1,0:T(2,128)(2,1)S(1)} %get-tuple-element.7639), channel_id=1, source_target_pairs={{0,1},{1,2},{2,3},{4,5},{5,6},{6,7},{8,9},{9,10},{10,11},{12,13},{... | collective-permute-start | bytes 196616 | tf_op jit(solution)/shard_map/ppermute | solution.py:15
  202.6 5.0 collective-permute-start.20
  207.8 8.5 %collective-permute-start.21 = (bf16[1,4,2,4096]{3,2,1,0:T(2,128)(2,1)S(1)}, bf16[1,4,2,4096]{3,2,1,0:T(2,128)(2,1)S(1)}, u32[]{:S(2)}, u32[]{:S(2)}) collective-permute-start(bf16[1,4,2,4096]{3,2,1,0:T(2,128)(2,1)S(1)} %get-tuple-element.4124), channel_id=1, source_target_pairs={{1,0},{2,1},{3,2},{5,4},{6,5},{7,6},{9,8},{10,9},{11,10},{13,12},{... | collective-permute-start | bytes 196616 | tf_op jit(solution)/shard_map/ppermute | solution.py:15
  216.4 5.6 collective-permute-start.22
  222.6 19.2 %collective-permute-start.23 = (bf16[1,4,2,4096]{3,2,1,0:T(2,128)(2,1)S(1)}, bf16[1,4,2,4096]{3,2,1,0:T(2,128)(2,1)S(1)}, u32[]{:S(2)}, u32[]{:S(2)}) collective-permute-start(bf16[1,4,2,4096]{3,2,1,0:T(2,128)(2,1)S(1)} %get-tuple-element.4128), channel_id=1, source_target_pairs={{1,0},{2,1},{3,2},{5,4},{6,5},{7,6},{9,8},{10,9},{11,10},{13,12},{... | collective-permute-start | bytes 196616 | tf_op jit(solution)/shard_map/ppermute | solution.py:15
  254.8 5.0 collective-permute-start.25
  263.8 5.2 collective-permute-start.26
  273.0 5.4 collective-permute-start.27
  282.3 5.0 collective-permute-start.28
  300.3 5.0 collective-permute-start.30
  309.3 5.0 collective-permute-start.31
  336.3 5.5 collective-permute-start.34
  345.9 5.9 collective-permute-start.35
  364.8 5.0 collective-permute-start.37
  374.0 5.0 collective-permute-start.38
  385.7 380.9 %all-gather.3.cloned.1.call-start = ((), (), s32[]{:S(2)}) async-start(), calls=%async_computation.1 | async-start | bytes 16809984 | tf_op jit(solution)/shard_map/all_gather | solution.py:212
  (11 other events, 56.9 us)
Sparse Core Ops, SparseCore 0:
  385.8 238.2 reduce-scatter.3
  629.2 137.4 all-gather.2
